TPU v7x, 32 devices: a whole 2x2x4 slice. The times are simulated.
32 devices in a mesh: inst: 4 (over z), shard: 8 (over y, x, core).
Axes of the slice: x: 2, y: 2, z: 4, core: 2. Of those that a mesh axis runs over, the one named last changes fastest.
Arguments:
- master_old: float32 [4, 16, 65536], P('inst', 'shard'), may hold values from -3 to 3
- first_old: float32 [4, 16, 65536], P('inst', 'shard'), may hold values from -2 to 2
- second_old: float32 [4, 16, 65536], P('inst', 'shard'), may hold values from 0.01 to 1
- healthy: int32 [8], replicated, may hold values from 0 to 3
- slice_table: int32 [16], replicated, may hold values from 0 to 15, as said below
Outputs:
- master_new: float32 [4, 16, 65536], P('inst', 'shard')
- first_new: float32 [4, 16, 65536], P('inst', 'shard')
- second_new: float32 [4, 16, 65536], P('inst', 'shard')
- params_half: bfloat16 [4, 16, 65536], P('inst', 'shard')
- checksum: float32 [4, 2], P('inst')
Inputs may be any that keep to these rules, and one draw needn't show every extreme that they name: slice_table[k] = (k + slice_table[0]) mod 16 for every k, with slice_table[0] odd and at least 3.
All inputs are finite; a program needn't handle non-finite values.
Results may differ from a plain program's by a relative error of at most 0.001.
Values sent between devices are 32-bit elements; how exact they have to be, the bound alone decides.
No kernel may reach another device: no remote copies, remote signals or barrier semaphores. Data moves between devices by JAX's collectives and lax.ppermute only.
A program may use at most 64 MiB of HBM per device.

v0:
```python
import jax
import jax.numpy as jnp
from jax import lax
from jax.sharding import PartitionSpec as P


def passed_along(value, axis, steps):
    count = lax.axis_size(axis)
    pairs = [(source, (source + steps) % count) for source in range(count)]
    return lax.ppermute(value, axis, pairs)


def from_root(block, axis, owner):
    block = jnp.where(lax.axis_index(axis) == owner, block, jnp.zeros_like(block))
    return lax.psum(block, axis)


def position_keys(flat_rows, columns):
    residue = flat_rows * (columns % 101) % 101
    offsets = jnp.arange(columns, dtype=jnp.int32)
    cycled = (residue[:, None] + offsets[None, :]) % 101
    return (cycled * 37 % 101 + 1).astype(jnp.float32) / 101.0


def weighted(master, first_moment, second, flat_rows):
    weights = position_keys(flat_rows, master.shape[2])
    combined = master[0] + first_moment[0] + second[0]
    return jnp.stack([jnp.sum(combined * weights), jnp.sum(master[0] * weights)])


def grand_total(partial_value):
    return lax.psum(partial_value, "shard")


def join_parts(pieces):
    return (
        lax.all_gather(pieces[0], "inst", axis=2, tiled=True),
        lax.all_gather(pieces[1], "inst", axis=2, tiled=True),
        lax.all_gather(pieces[2], "inst", axis=2, tiled=True),
    )


def reorder(arrays, rotation, owners):
    for bit_level in range((owners - 1).bit_length()):
        shifted = passed_along((arrays[0], arrays[1], arrays[2]), "shard", 1 << bit_level)
        chosen = rotation >> bit_level & 1 == 1
        arrays = tuple(
            (
                jnp.where(chosen, shifted_one, current)
                for shifted_one, current in zip(shifted, arrays)
            )
        )
    carried = passed_along((arrays[0][:, 1:2], arrays[1][:, 1:2], arrays[2][:, 1:2]), "shard", 1)
    return tuple(
        (
            jnp.concatenate([carried_one, current[:, 0:1]], axis=1)
            for carried_one, current in zip(carried, arrays)
        )
    )


def on_device(master_old, first_old, second_old, healthy, slice_table):
    source_index = lax.dynamic_index_in_dim(healthy, lax.axis_index("shard"), 0, keepdims=False)
    owners = lax.axis_size("shard")
    instances = lax.axis_size("inst")
    columns = master_old.shape[2]
    part_len = columns // instances
    normalizer = 1.0 / (2.0 * columns)
    rotation = slice_table[0] // 2
    master, first_moment, second = (
        from_root(master_old, "inst", source_index),
        from_root(first_old, "inst", source_index),
        from_root(second_old, "inst", source_index),
    )
    offset_start = lax.axis_index("inst") * part_len
    pieces = tuple(
        (
            lax.dynamic_slice_in_dim(stacked, offset_start, part_len, 2)
            for stacked in (master, first_moment, second)
        )
    )
    pieces = reorder(pieces, rotation, owners)
    master, first_moment, second = join_parts(pieces)
    new_rows = 2 * lax.axis_index("shard") + jnp.arange(2, dtype=jnp.int32)
    checksum = grand_total(weighted(master, first_moment, second, new_rows))
    checksum = jnp.reshape(checksum * normalizer, (1, 2))
    return (master, first_moment, second, master.astype(jnp.bfloat16), checksum)


def solution(mesh):
    placed = (
        P("inst", "shard", None),
        P("inst", "shard", None),
        P("inst", "shard", None),
        P(),
        P(),
    )
    return jax.shard_map(
        on_device,
        mesh=mesh,
        in_specs=placed,
        out_specs=(
            P("inst", "shard", None),
            P("inst", "shard", None),
            P("inst", "shard", None),
            P("inst", "shard", None),
            P("inst", None),
        ),
        check_vma=False,
    )
```

profile of v0, /device:TPU:0, one launch (start us, length us, event | category | flops | bytes accessed | tf_op | source)
XLA Modules:
  0.0 187.4 jit_solution(15723886663687752897)
XLA Ops:
  9.1 2.1 %broadcast_select_fusion.2 = f32[1,2,65536]{2,1,0:T(2,128)} fusion(f32[1,2,65536]{2,1,0:T(2,128)} %param.5, pred[]{:T(512)S(6)} %eq.22), kind=kLoop, calls=%fused_computation.15 | loop fusion | flops 131072 | bytes 1048577 | tf_op jit(solution)/shard_map/jit(_where)/select_n | solution.py:14
  11.3 1.5 broadcast_select_fusion
  13.7 70.2 %all-reduce.3.cloned.1.call-done = (f32[1,2,65536]{2,1,0:T(2,128)}, f32[1,2,65536]{2,1,0:T(2,128)}, f32[1,2,65536]{2,1,0:T(2,128)}) async-done(((f32[1,2,65536]{2,1,0:T(2,128)}, f32[1,2,65536]{2,1,0:T(2,128)}, f32[1,2,65536]{2,1,0:T(2,128)}), (f32[1,2,65536]{2,1,0:T(2,128)}, f32[1,2,65536]{2,1,0:T(2,128)}, f32[1,2,65536]{2,1,0:T(2,128)})) %all-reduce.3.cloned.1.call-update) | async-done | bytes 1572880 | tf_op jit(solution)/shard_map/psum | solution.py:15
  83.9 1.0 constant_dynamic-slice_fusion
  84.9 0.9 constant_dynamic-slice_fusion.1
  85.8 1.6 collective-permute-start.4
  87.6 2.6 %collective-permute-done.8 = f32[1,2,16384]{2,1,0:T(2,128)S(1)} collective-permute-done((f32[1,2,16384]{2,1,0:T(2,128)S(1)}, f32[1,2,16384]{2,1,0:T(2,128)S(1)}, u32[]{:S(2)}, u32[]{:S(2)}) %collective-permute-start.8) | collective-permute-done | bytes 131104 | tf_op jit(solution)/shard_map/ppermute | solution.py:10
  90.2 1.0 broadcast_select_fusion.3
  91.8 1.0 broadcast_select_fusion.4
  92.8 2.4 %collective-permute-start.5 = (f32[1,2,16384]{2,1,0:T(2,128)S(1)}, f32[1,2,16384]{2,1,0:T(2,128)S(1)}, u32[]{:S(2)}, u32[]{:S(2)}) collective-permute-start(f32[1,2,16384]{2,1,0:T(2,128)S(1)} %broadcast_select_fusion.4), channel_id=1, source_target_pairs={{0,2},{1,3},{2,4},{3,5},{4,6},{5,7},{6,0},{7,1},{8,10},{9,11},{10,... | collective-permute-start | bytes 393224 | tf_op jit(solution)/shard_map/ppermute | solution.py:10
  95.9 2.5 %collective-permute-done.9 = f32[1,2,16384]{2,1,0:T(2,128)S(1)} collective-permute-done((f32[1,2,16384]{2,1,0:T(2,128)S(1)}, f32[1,2,16384]{2,1,0:T(2,128)S(1)}, u32[]{:S(2)}, u32[]{:S(2)}) %collective-permute-start.9) | collective-permute-done | bytes 131104 | tf_op jit(solution)/shard_map/ppermute | solution.py:10
  98.5 1.7 collective-permute-start.10
  100.2 1.0 collective-permute-done.5
  101.3 1.0 collective-permute-start.6
  103.7 1.9 %collective-permute-done.10 = f32[1,2,16384]{2,1,0:T(2,128)S(1)} collective-permute-done((f32[1,2,16384]{2,1,0:T(2,128)S(1)}, f32[1,2,16384]{2,1,0:T(2,128)S(1)}, u32[]{:S(2)}, u32[]{:S(2)}) %collective-permute-start.10) | collective-permute-done | bytes 131104 | tf_op jit(solution)/shard_map/ppermute | solution.py:10
  105.9 2.6 %collective-permute-done.6 = f32[1,2,16384]{2,1,0:T(2,128)S(1)} collective-permute-done((f32[1,2,16384]{2,1,0:T(2,128)S(1)}, f32[1,2,16384]{2,1,0:T(2,128)S(1)}, u32[]{:S(2)}, u32[]{:S(2)}) %collective-permute-start.6) | collective-permute-done | bytes 131104 | tf_op jit(solution)/shard_map/ppermute | solution.py:10
  108.7 3.2 %collective-permute-done.2 = f32[1,2,16384]{2,1,0:T(2,128)S(1)} collective-permute-done((f32[1,2,16384]{2,1,0:T(2,128)S(1)}, f32[1,2,16384]{2,1,0:T(2,128)S(1)}, u32[]{:S(2)}, u32[]{:S(2)}) %collective-permute-start.2) | collective-permute-done | bytes 131104 | tf_op jit(solution)/shard_map/ppermute | solution.py:10
  112.2 16.1 %all_gather.11 = f32[1,2,65536]{2,1,0:T(2,128)S(1)} all-gather(f32[1,2,16384]{2,1,0:T(2,128)S(1)} %pad_maximum_fusion.2), channel_id=1, replica_groups=mesh['inst'=4,'shard'=8] {'inst'}, dimensions={2}, use_global_device_ids=true | all-gather | bytes 655360 | tf_op jit(solution)/shard_map/all_gather | solution.py:39
  128.4 15.8 %all_gather.10 = f32[1,2,65536]{2,1,0:T(2,128)S(1)} all-gather(f32[1,2,16384]{2,1,0:T(2,128)S(1)} %pad_maximum_fusion.1), channel_id=1, replica_groups=mesh['inst'=4,'shard'=8] {'inst'}, dimensions={2}, use_global_device_ids=true | all-gather | bytes 655360 | tf_op jit(solution)/shard_map/all_gather | solution.py:38
  144.3 15.0 %all_gather.9 = f32[1,2,65536]{2,1,0:T(2,128)S(1)} all-gather(f32[1,2,16384]{2,1,0:T(2,128)S(1)} %pad_maximum_fusion), channel_id=1, replica_groups=mesh['inst'=4,'shard'=8] {'inst'}, dimensions={2}, use_global_device_ids=true | all-gather | bytes 655360 | tf_op jit(solution)/shard_map/all_gather | solution.py:37
  159.3 4.3 %fusion.6 = (f32[]{:T(128)}, f32[]{:T(128)}) fusion(f32[1,2,65536]{2,1,0:T(2,128)S(1)} %all_gather.11, f32[1,2,65536]{2,1,0:T(2,128)S(1)} %all_gather.10, f32[1,2,65536]{2,1,0:T(2,128)S(1)} %all_gather.9, s32[2]{0:T(128)S(1)} %and_select_fusion.2), kind=kLoop, calls=%fused_computation.9 | loop fusion | flops 3014654 | bytes 1572880 | tf_op jit(solution)/shard_map/reduce_sum | solution.py:28
  163.6 1.4 pad_maximum_fusion.3
  165.0 0.9 convert_element_type.6
  165.9 11.8 %psum.31 = f32[2]{0:T(128)S(1)} all-reduce(f32[2]{0:T(128)S(1)} %pad_maximum_fusion.3), channel_id=1, replica_groups=mesh['inst'=4,'shard'=8] {'shard'}, use_global_device_ids=true, to_apply=%region_5.6 | all-reduce | flops 2 | bytes 16 | tf_op jit(solution)/shard_map/psum | solution.py:32
  (46 shorter events, 8.9 us)
Async XLA Ops:
  7.2 76.7 %all-reduce.3.cloned.1.call-start = ((), (), s32[]{:S(2)}) async-start(), calls=%async_computation | async-start | bytes 3145728 | tf_op jit(solution)/shard_map/psum | solution.py:15
  7.2 0.7 copy-start.4
  9.1 2.2 %copy-start = (f32[1,2,65536]{2,1,0:T(2,128)S(1)}, f32[1,2,65536]{2,1,0:T(2,128)}, u32[]{:S(2)}) copy-start(f32[1,2,65536]{2,1,0:T(2,128)} %param.7) | copy-start | bytes 1572868
  9.1 2.2 %copy-start.1 = (f32[1,2,65536]{2,1,0:T(2,128)S(1)}, f32[1,2,65536]{2,1,0:T(2,128)}, u32[]{:S(2)}) copy-start(f32[1,2,65536]{2,1,0:T(2,128)} %param.6) | copy-start | bytes 1572868
  12.8 0.7 copy-start.3
  83.9 3.6 %copy-start.2 = (f32[1,2,65536]{2,1,0:T(2,128)S(1)}, f32[1,2,65536]{2,1,0:T(2,128)}, u32[]{:S(2)}) copy-start(f32[1,2,65536]{2,1,0:T(2,128)} %get-tuple-element.7) | copy-start | bytes 1572868
  84.9 5.3 %collective-permute-start.8 = (f32[1,2,16384]{2,1,0:T(2,128)S(1)}, f32[1,2,16384]{2,1,0:T(2,128)S(1)}, u32[]{:S(2)}, u32[]{:S(2)}) collective-permute-start(f32[1,2,16384]{2,1,0:T(2,128)S(1)} %constant_dynamic-slice_fusion), channel_id=1, source_target_pairs={{0,1},{1,2},{2,3},{3,4},{4,5},{5,6},{6,7},{7,0},{8,9},{9,10},{10,1... | collective-permute-start | bytes 393224 | tf_op jit(solution)/shard_map/ppermute | solution.py:10
  85.8 6.0 %collective-permute-start.4 = (f32[1,2,16384]{2,1,0:T(2,128)S(1)}, f32[1,2,16384]{2,1,0:T(2,128)S(1)}, u32[]{:S(2)}, u32[]{:S(2)}) collective-permute-start(f32[1,2,16384]{2,1,0:T(2,128)S(1)} %constant_dynamic-slice_fusion.1), channel_id=1, source_target_pairs={{0,1},{1,2},{2,3},{3,4},{4,5},{5,6},{6,7},{7,0},{8,9},{9,10},{10,1... | collective-permute-start | bytes 393224 | tf_op jit(solution)/shard_map/ppermute | solution.py:10
  87.5 7.7 %collective-permute-start = (f32[1,2,16384]{2,1,0:T(2,128)S(1)}, f32[1,2,16384]{2,1,0:T(2,128)S(1)}, u32[]{:S(2)}, u32[]{:S(2)}) collective-permute-start(f32[1,2,16384]{2,1,0:T(2,128)S(1)} %constant_dynamic-slice_fusion.2), channel_id=1, source_target_pairs={{0,1},{1,2},{2,3},{3,4},{4,5},{5,6},{6,7},{7,0},{8,9},{9,10},{10,1... | collective-permute-start | bytes 393224 | tf_op jit(solution)/shard_map/ppermute | solution.py:10
  91.2 7.2 %collective-permute-start.9 = (f32[1,2,16384]{2,1,0:T(2,128)S(1)}, f32[1,2,16384]{2,1,0:T(2,128)S(1)}, u32[]{:S(2)}, u32[]{:S(2)}) collective-permute-start(f32[1,2,16384]{2,1,0:T(2,128)S(1)} %broadcast_select_fusion.3), channel_id=1, source_target_pairs={{0,2},{1,3},{2,4},{3,5},{4,6},{5,7},{6,0},{7,1},{8,10},{9,11},{10,... | collective-permute-start | bytes 393224 | tf_op jit(solution)/shard_map/ppermute | solution.py:10
  92.8 8.5 %collective-permute-start.5 = (f32[1,2,16384]{2,1,0:T(2,128)S(1)}, f32[1,2,16384]{2,1,0:T(2,128)S(1)}, u32[]{:S(2)}, u32[]{:S(2)}) collective-permute-start(f32[1,2,16384]{2,1,0:T(2,128)S(1)} %broadcast_select_fusion.4), channel_id=1, source_target_pairs={{0,2},{1,3},{2,4},{3,5},{4,6},{5,7},{6,0},{7,1},{8,10},{9,11},{10,... | collective-permute-start | bytes 393224 | tf_op jit(solution)/shard_map/ppermute | solution.py:10
  95.3 7.5 %collective-permute-start.1 = (f32[1,2,16384]{2,1,0:T(2,128)S(1)}, f32[1,2,16384]{2,1,0:T(2,128)S(1)}, u32[]{:S(2)}, u32[]{:S(2)}) collective-permute-start(f32[1,2,16384]{2,1,0:T(2,128)S(1)} %broadcast_select_fusion.5), channel_id=1, source_target_pairs={{0,2},{1,3},{2,4},{3,5},{4,6},{5,7},{6,0},{7,1},{8,10},{9,11},{10,... | collective-permute-start | bytes 393224 | tf_op jit(solution)/shard_map/ppermute | solution.py:10
  98.5 7.1 %collective-permute-start.10 = (f32[1,2,16384]{2,1,0:T(2,128)S(1)}, f32[1,2,16384]{2,1,0:T(2,128)S(1)}, u32[]{:S(2)}, u32[]{:S(2)}) collective-permute-start(f32[1,2,16384]{2,1,0:T(2,128)S(1)} %broadcast_select_fusion.6), channel_id=1, source_target_pairs={{0,4},{1,5},{2,6},{3,7},{4,0},{5,1},{6,2},{7,3},{8,12},{9,13},{10,... | collective-permute-start | bytes 393224 | tf_op jit(solution)/shard_map/ppermute | solution.py:10
  101.3 7.1 %collective-permute-start.6 = (f32[1,2,16384]{2,1,0:T(2,128)S(1)}, f32[1,2,16384]{2,1,0:T(2,128)S(1)}, u32[]{:S(2)}, u32[]{:S(2)}) collective-permute-start(f32[1,2,16384]{2,1,0:T(2,128)S(1)} %broadcast_select_fusion.7), channel_id=1, source_target_pairs={{0,4},{1,5},{2,6},{3,7},{4,0},{5,1},{6,2},{7,3},{8,12},{9,13},{10,... | collective-permute-start | bytes 393224 | tf_op jit(solution)/shard_map/ppermute | solution.py:10
  102.9 9.0 %collective-permute-start.2 = (f32[1,2,16384]{2,1,0:T(2,128)S(1)}, f32[1,2,16384]{2,1,0:T(2,128)S(1)}, u32[]{:S(2)}, u32[]{:S(2)}) collective-permute-start(f32[1,2,16384]{2,1,0:T(2,128)S(1)} %broadcast_select_fusion.8), channel_id=1, source_target_pairs={{0,4},{1,5},{2,6},{3,7},{4,0},{5,1},{6,2},{7,3},{8,12},{9,13},{10,... | collective-permute-start | bytes 393224 | tf_op jit(solution)/shard_map/ppermute | solution.py:10
  105.8 6.3 %collective-permute-start.11 = (f32[1,1,16384]{2,1,0:T(1,128)S(1)}, f32[1,1,16384]{2,1,0:T(1,128)S(1)}, u32[]{:S(2)}, u32[]{:S(2)}) collective-permute-start(f32[1,1,16384]{2,1,0:T(1,128)S(1)} %get-tuple-element.10), channel_id=1, source_target_pairs={{0,1},{1,2},{2,3},{3,4},{4,5},{5,6},{6,7},{7,0},{8,9},{9,10},{10,1... | collective-permute-start | bytes 196616 | tf_op jit(solution)/shard_map/ppermute | solution.py:10
  108.6 19.7 %collective-permute-start.7 = (f32[1,1,16384]{2,1,0:T(1,128)S(1)}, f32[1,1,16384]{2,1,0:T(1,128)S(1)}, u32[]{:S(2)}, u32[]{:S(2)}) collective-permute-start(f32[1,1,16384]{2,1,0:T(1,128)S(1)} %get-tuple-element.12), channel_id=1, source_target_pairs={{0,1},{1,2},{2,3},{3,4},{4,5},{5,6},{6,7},{7,0},{8,9},{9,10},{10,1... | collective-permute-start | bytes 196616 | tf_op jit(solution)/shard_map/ppermute | solution.py:10
  112.0 32.2 %collective-permute-start.3 = (f32[1,1,16384]{2,1,0:T(1,128)S(1)}, f32[1,1,16384]{2,1,0:T(1,128)S(1)}, u32[]{:S(2)}, u32[]{:S(2)}) collective-permute-start(f32[1,1,16384]{2,1,0:T(1,128)S(1)} %get-tuple-element.14), channel_id=1, source_target_pairs={{0,1},{1,2},{2,3},{3,4},{4,5},{5,6},{6,7},{7,0},{8,9},{9,10},{10,1... | collective-permute-start | bytes 196616 | tf_op jit(solution)/shard_map/ppermute | solution.py:10
Sparse Core Ops, SparseCore 0:
  12.9 70.8 all-reduce.2
where the time goes:
time: 188 us; the launch traced here: 187 us
  waiting for transfers between devices  84.6 us (45%)
  blocking collectives  58.6 us (31%)
  between operations  15 us (8%)
  other arithmetic  13.5 us (7%)
  starting transfers between devices  9.11 us (5%)
  local copies, waits for them, and re-layouts  6.49 us (3%)
    psum x1, waiting for transfers between devices, from_root(): return lax.psum(block, axis)  70.2 us
    all_gather x1, blocking collectives, join_parts(): lax.all_gather(pieces[2], 'inst', axis=2, tiled=True)  16.1 us
    all_gather x1, blocking collectives, join_parts(): lax.all_gather(pieces[1], 'inst', axis=2, tiled=True)  15.8 us
    all_gather x1, blocking collectives, join_parts(): lax.all_gather(pieces[0], 'inst', axis=2, tiled=True)  15 us
    ppermute x12, waiting for transfers between devices, passed_along(): return lax.ppermute(value, axis, pairs)  14.4 us
    psum x1, blocking collectives, grand_total(): return lax.psum(partial_value, 'shard')  11.8 us
    ppermute x12, starting transfers between devices, passed_along(): return lax.ppermute(value, axis, pairs)  9.07 us
    reduce_sum x1, other arithmetic, weighted(): jnp.sum(combined * weights)  4.28 us
  transfers between devices with their start and end apart: 13, of which 8 were waited for; matrix products, arithmetic and copies ran while one was open for 2% of the time, Pallas kernels for 0%

commit v1 on v0

--- a/solution.py
+++ b/solution.py
@@ -1,7 +1,29 @@
+import functools
 import jax
 import jax.numpy as jnp
 from jax import lax
 from jax.sharding import PartitionSpec as P
+
+
+def report_axis_part(arr_in, lane_axis):
+    small, block_now, o_now = (lax.axis_size(lane_axis), lax.axis_index(lane_axis), arr_in.shape[2])
+    n_now, clean = (arr_in, 1)
+    while clean < small:
+        n_now = jnp.concatenate(
+            [
+                n_now,
+                lax.ppermute(
+                    n_now, lane_axis, [(nth, (nth - clean) % small) for nth in range(small)]
+                ),
+            ],
+            axis=2,
+        )
+        clean = 2 * clean
+    current_value = jnp.roll(n_now, shift=block_now * o_now, axis=2)
+    return current_value
+
+
+point_sites = functools.partial(report_axis_part, lane_axis="inst")
 
 
 def passed_along(value, axis, steps):
@@ -36,7 +58,7 @@
     return (
         lax.all_gather(pieces[0], "inst", axis=2, tiled=True),
         lax.all_gather(pieces[1], "inst", axis=2, tiled=True),
-        lax.all_gather(pieces[2], "inst", axis=2, tiled=True),
+        point_sites(pieces[2]),
     )
 
 

time: 188 us -> 185 us (0.984)
  blocking collectives: 58.6 us -> 43.8 us
  waiting for transfers between devices: 84.6 us -> 93.8 us
  starting transfers between devices: 9.11 us -> 11.7 us
    all_gather x1 -> x0, blocking collectives: 16.1 us -> none  [join_parts(): lax.all_gather(pieces[2], 'inst', axis=2, tiled=True)]
    ppermute x0 -> x2, waiting for transfers between devices: none -> 9.15 us  [report_axis_part(): lax.ppermute(n_now, lane_axis, [(nth, (nth - clean) % small) for nth in r...]
    ppermute x0 -> x2, starting transfers between devices: none -> 2.55 us  [report_axis_part(): lax.ppermute(n_now, lane_axis, [(nth, (nth - clean) % small) for nth in r...]
  transfers between devices with their start and end apart: 13 -> 15, of which waited for: 8 -> 9; matrix products, arithmetic and copies ran while one was open for 2% -> 2% of each run, Pallas kernels for 0% -> 0%
where the time goes in v1:
time: 185 us
  waiting for transfers between devices  93.8 us (51%)
  blocking collectives  43.8 us (24%)
  between operations  15.1 us (8%)
  other arithmetic  14.4 us (8%)
  starting transfers between devices  11.7 us (6%)
  local copies, waits for them, and re-layouts  5.8 us (3%)
    psum x1, waiting for transfers between devices, from_root(): return lax.psum(block, axis)  70.2 us
    all_gather x1, blocking collectives, join_parts(): lax.all_gather(pieces[0], 'inst', axis=2, tiled=True)  15.9 us
    all_gather x1, blocking collectives, join_parts(): lax.all_gather(pieces[1], 'inst', axis=2, tiled=True)  15.1 us
    ppermute x12, waiting for transfers between devices, passed_along(): return lax.ppermute(value, axis, pairs)  14.4 us
    psum x1, blocking collectives, grand_total(): return lax.psum(partial_value, 'shard')  12.8 us
    ppermute x2, waiting for transfers between devices, report_axis_part(): lax.ppermute(n_now, lane_axis, [(nth, (nth - clean) % small) for nth in r...  9.15 us
    ppermute x12, starting transfers between devices, passed_along(): return lax.ppermute(value, axis, pairs)  9.07 us
    reduce_sum x1, other arithmetic, weighted(): jnp.sum(combined * weights)  4.88 us
  transfers between devices with their start and end apart: 15, of which 9 were waited for; matrix products, arithmetic and copies ran while one was open for 2% of the time, Pallas kernels for 0%

profile of v1, /device:TPU:0, one launch (start us, length us, event | category | flops | bytes accessed | tf_op | source)
XLA Modules:
  0.0 184.6 jit_solution(14972836048192419077)
XLA Ops:
  9.1 2.1 %broadcast_select_fusion.2 = f32[1,2,65536]{2,1,0:T(2,128)} fusion(f32[1,2,65536]{2,1,0:T(2,128)} %param.5, pred[]{:T(512)S(6)} %eq.25), kind=kLoop, calls=%fused_computation.15 | loop fusion | flops 131072 | bytes 1048577 | tf_op jit(solution)/shard_map/jit(_where)/select_n | solution.py:36
  11.3 1.5 broadcast_select_fusion
  13.7 70.2 %all-reduce.3.cloned.1.call-done = (f32[1,2,65536]{2,1,0:T(2,128)}, f32[1,2,65536]{2,1,0:T(2,128)}, f32[1,2,65536]{2,1,0:T(2,128)}) async-done(((f32[1,2,65536]{2,1,0:T(2,128)}, f32[1,2,65536]{2,1,0:T(2,128)}, f32[1,2,65536]{2,1,0:T(2,128)}), (f32[1,2,65536]{2,1,0:T(2,128)}, f32[1,2,65536]{2,1,0:T(2,128)}, f32[1,2,65536]{2,1,0:T(2,128)})) %all-reduce.3.cloned.1.call-update) | async-done | bytes 1572880 | tf_op jit(solution)/shard_map/psum | solution.py:37
  83.9 1.0 constant_dynamic-slice_fusion.1
  85.8 1.6 collective-permute-start.4
  87.6 2.6 %collective-permute-done.8 = f32[1,2,16384]{2,1,0:T(2,128)S(1)} collective-permute-done((f32[1,2,16384]{2,1,0:T(2,128)S(1)}, f32[1,2,16384]{2,1,0:T(2,128)S(1)}, u32[]{:S(2)}, u32[]{:S(2)}) %collective-permute-start.8) | collective-permute-done | bytes 131104 | tf_op jit(solution)/shard_map/ppermute | solution.py:32
  90.2 1.0 broadcast_select_fusion.3
  91.8 1.0 broadcast_select_fusion.4
  92.8 2.4 %collective-permute-start.5 = (f32[1,2,16384]{2,1,0:T(2,128)S(1)}, f32[1,2,16384]{2,1,0:T(2,128)S(1)}, u32[]{:S(2)}, u32[]{:S(2)}) collective-permute-start(f32[1,2,16384]{2,1,0:T(2,128)S(1)} %broadcast_select_fusion.4), channel_id=1, source_target_pairs={{0,2},{1,3},{2,4},{3,5},{4,6},{5,7},{6,0},{7,1},{8,10},{9,11},{10,... | collective-permute-start | bytes 393224 | tf_op jit(solution)/shard_map/ppermute | solution.py:32
  95.9 2.5 %collective-permute-done.9 = f32[1,2,16384]{2,1,0:T(2,128)S(1)} collective-permute-done((f32[1,2,16384]{2,1,0:T(2,128)S(1)}, f32[1,2,16384]{2,1,0:T(2,128)S(1)}, u32[]{:S(2)}, u32[]{:S(2)}) %collective-permute-start.9) | collective-permute-done | bytes 131104 | tf_op jit(solution)/shard_map/ppermute | solution.py:32
  98.5 1.7 collective-permute-start.10
  100.2 1.0 collective-permute-done.5
  101.3 1.0 collective-permute-start.6
  103.7 1.9 %collective-permute-done.10 = f32[1,2,16384]{2,1,0:T(2,128)S(1)} collective-permute-done((f32[1,2,16384]{2,1,0:T(2,128)S(1)}, f32[1,2,16384]{2,1,0:T(2,128)S(1)}, u32[]{:S(2)}, u32[]{:S(2)}) %collective-permute-start.10) | collective-permute-done | bytes 131104 | tf_op jit(solution)/shard_map/ppermute | solution.py:32
  105.9 2.6 %collective-permute-done.6 = f32[1,2,16384]{2,1,0:T(2,128)S(1)} collective-permute-done((f32[1,2,16384]{2,1,0:T(2,128)S(1)}, f32[1,2,16384]{2,1,0:T(2,128)S(1)}, u32[]{:S(2)}, u32[]{:S(2)}) %collective-permute-start.6) | collective-permute-done | bytes 131104 | tf_op jit(solution)/shard_map/ppermute | solution.py:32
  108.7 3.2 %collective-permute-done.2 = f32[1,2,16384]{2,1,0:T(2,128)S(1)} collective-permute-done((f32[1,2,16384]{2,1,0:T(2,128)S(1)}, f32[1,2,16384]{2,1,0:T(2,128)S(1)}, u32[]{:S(2)}, u32[]{:S(2)}) %collective-permute-start.2) | collective-permute-done | bytes 131104 | tf_op jit(solution)/shard_map/ppermute | solution.py:32
  112.3 1.6 collective-permute-start.12
  113.9 15.1 %all_gather.7 = f32[1,2,65536]{2,1,0:T(2,128)S(1)} all-gather(f32[1,2,16384]{2,1,0:T(2,128)S(1)} %pad_maximum_fusion.2), channel_id=1, replica_groups=mesh['inst'=4,'shard'=8] {'inst'}, dimensions={2}, use_global_device_ids=true | all-gather | bytes 655360 | tf_op jit(solution)/shard_map/all_gather | solution.py:60
  129.2 15.9 %all_gather.6 = f32[1,2,65536]{2,1,0:T(2,128)S(1)} all-gather(f32[1,2,16384]{2,1,0:T(2,128)S(1)} %pad_maximum_fusion.1), channel_id=1, replica_groups=mesh['inst'=4,'shard'=8] {'inst'}, dimensions={2}, use_global_device_ids=true | all-gather | bytes 655360 | tf_op jit(solution)/shard_map/all_gather | solution.py:59
  145.3 1.0 collective-permute-start.13
  146.3 9.1 %collective-permute-done.13 = f32[1,2,32768]{2,1,0:T(2,128)S(1)} collective-permute-done((f32[1,2,32768]{2,1,0:T(2,128)S(1)}, f32[1,2,32768]{2,1,0:T(2,128)S(1)}, u32[]{:S(2)}, u32[]{:S(2)}) %collective-permute-start.13) | collective-permute-done | bytes 262176 | tf_op jit(solution)/shard_map/ppermute | solution.py:15
  155.7 4.9 %fusion.6 = (f32[]{:T(128)}, f32[]{:T(128)}, f32[1,2,65536]{2,1,0:T(2,128)}) fusion(f32[1,2,65536]{2,1,0:T(2,128)S(1)} %all_gather.7, f32[1,2,65536]{2,1,0:T(2,128)S(1)} %all_gather.6, s32[2]{0:T(128)S(1)} %and_select_fusion.2, f32[1,2,131072]{2,1,0:T(2,128)S(1)} %constant_dynamic-update-slice_fusion, s32[]{:T(128)S(6)} %select_n.126), kind=kLoop, calls=%fused_computation.9 | loop fusion | flops 3014654 | bytes 2097172 | tf_op jit(solution)/shard_map/reduce_sum | solution.py:50
  160.6 1.4 pad_maximum_fusion.4
  162.8 12.8 %psum.31 = f32[2]{0:T(128)S(1)} all-reduce(f32[2]{0:T(128)S(1)} %pad_maximum_fusion.4), channel_id=1, replica_groups=mesh['inst'=4,'shard'=8] {'shard'}, use_global_device_ids=true, to_apply=%region_5.6 | all-reduce | flops 2 | bytes 16 | tf_op jit(solution)/shard_map/psum | solution.py:54
  (54 shorter events, 10.4 us)
Async XLA Ops:
  7.2 76.7 %all-reduce.3.cloned.1.call-start = ((), (), s32[]{:S(2)}) async-start(), calls=%async_computation | async-start | bytes 3145728 | tf_op jit(solution)/shard_map/psum | solution.py:37
  7.2 0.7 copy-start.4
  9.1 2.2 %copy-start = (f32[1,2,65536]{2,1,0:T(2,128)S(1)}, f32[1,2,65536]{2,1,0:T(2,128)}, u32[]{:S(2)}) copy-start(f32[1,2,65536]{2,1,0:T(2,128)} %param.7) | copy-start | bytes 1572868
  9.1 2.2 %copy-start.1 = (f32[1,2,65536]{2,1,0:T(2,128)S(1)}, f32[1,2,65536]{2,1,0:T(2,128)}, u32[]{:S(2)}) copy-start(f32[1,2,65536]{2,1,0:T(2,128)} %param.6) | copy-start | bytes 1572868
  12.8 0.7 copy-start.3
  83.9 3.6 %copy-start.2 = (f32[1,2,65536]{2,1,0:T(2,128)S(1)}, f32[1,2,65536]{2,1,0:T(2,128)}, u32[]{:S(2)}) copy-start(f32[1,2,65536]{2,1,0:T(2,128)} %get-tuple-element.7) | copy-start | bytes 1572868
  84.9 5.3 %collective-permute-start.8 = (f32[1,2,16384]{2,1,0:T(2,128)S(1)}, f32[1,2,16384]{2,1,0:T(2,128)S(1)}, u32[]{:S(2)}, u32[]{:S(2)}) collective-permute-start(f32[1,2,16384]{2,1,0:T(2,128)S(1)} %constant_dynamic-slice_fusion.1), channel_id=1, source_target_pairs={{0,1},{1,2},{2,3},{3,4},{4,5},{5,6},{6,7},{7,0},{8,9},{9,10},{10,1... | collective-permute-start | bytes 393224 | tf_op jit(solution)/shard_map/ppermute | solution.py:32
  85.8 6.0 %collective-permute-start.4 = (f32[1,2,16384]{2,1,0:T(2,128)S(1)}, f32[1,2,16384]{2,1,0:T(2,128)S(1)}, u32[]{:S(2)}, u32[]{:S(2)}) collective-permute-start(f32[1,2,16384]{2,1,0:T(2,128)S(1)} %constant_dynamic-slice_fusion.2), channel_id=1, source_target_pairs={{0,1},{1,2},{2,3},{3,4},{4,5},{5,6},{6,7},{7,0},{8,9},{9,10},{10,1... | collective-permute-start | bytes 393224 | tf_op jit(solution)/shard_map/ppermute | solution.py:32
  87.5 7.7 %collective-permute-start = (f32[1,2,16384]{2,1,0:T(2,128)S(1)}, f32[1,2,16384]{2,1,0:T(2,128)S(1)}, u32[]{:S(2)}, u32[]{:S(2)}) collective-permute-start(f32[1,2,16384]{2,1,0:T(2,128)S(1)} %constant_dynamic-slice_fusion.3), channel_id=1, source_target_pairs={{0,1},{1,2},{2,3},{3,4},{4,5},{5,6},{6,7},{7,0},{8,9},{9,10},{10,1... | collective-permute-start | bytes 393224 | tf_op jit(solution)/shard_map/ppermute | solution.py:32
  91.2 7.2 %collective-permute-start.9 = (f32[1,2,16384]{2,1,0:T(2,128)S(1)}, f32[1,2,16384]{2,1,0:T(2,128)S(1)}, u32[]{:S(2)}, u32[]{:S(2)}) collective-permute-start(f32[1,2,16384]{2,1,0:T(2,128)S(1)} %broadcast_select_fusion.3), channel_id=1, source_target_pairs={{0,2},{1,3},{2,4},{3,5},{4,6},{5,7},{6,0},{7,1},{8,10},{9,11},{10,... | collective-permute-start | bytes 393224 | tf_op jit(solution)/shard_map/ppermute | solution.py:32
  92.8 8.5 %collective-permute-start.5 = (f32[1,2,16384]{2,1,0:T(2,128)S(1)}, f32[1,2,16384]{2,1,0:T(2,128)S(1)}, u32[]{:S(2)}, u32[]{:S(2)}) collective-permute-start(f32[1,2,16384]{2,1,0:T(2,128)S(1)} %broadcast_select_fusion.4), channel_id=1, source_target_pairs={{0,2},{1,3},{2,4},{3,5},{4,6},{5,7},{6,0},{7,1},{8,10},{9,11},{10,... | collective-permute-start | bytes 393224 | tf_op jit(solution)/shard_map/ppermute | solution.py:32
  95.3 7.5 %collective-permute-start.1 = (f32[1,2,16384]{2,1,0:T(2,128)S(1)}, f32[1,2,16384]{2,1,0:T(2,128)S(1)}, u32[]{:S(2)}, u32[]{:S(2)}) collective-permute-start(f32[1,2,16384]{2,1,0:T(2,128)S(1)} %broadcast_select_fusion.5), channel_id=1, source_target_pairs={{0,2},{1,3},{2,4},{3,5},{4,6},{5,7},{6,0},{7,1},{8,10},{9,11},{10,... | collective-permute-start | bytes 393224 | tf_op jit(solution)/shard_map/ppermute | solution.py:32
  98.5 7.1 %collective-permute-start.10 = (f32[1,2,16384]{2,1,0:T(2,128)S(1)}, f32[1,2,16384]{2,1,0:T(2,128)S(1)}, u32[]{:S(2)}, u32[]{:S(2)}) collective-permute-start(f32[1,2,16384]{2,1,0:T(2,128)S(1)} %broadcast_select_fusion.6), channel_id=1, source_target_pairs={{0,4},{1,5},{2,6},{3,7},{4,0},{5,1},{6,2},{7,3},{8,12},{9,13},{10,... | collective-permute-start | bytes 393224 | tf_op jit(solution)/shard_map/ppermute | solution.py:32
  101.3 7.1 %collective-permute-start.6 = (f32[1,2,16384]{2,1,0:T(2,128)S(1)}, f32[1,2,16384]{2,1,0:T(2,128)S(1)}, u32[]{:S(2)}, u32[]{:S(2)}) collective-permute-start(f32[1,2,16384]{2,1,0:T(2,128)S(1)} %broadcast_select_fusion.7), channel_id=1, source_target_pairs={{0,4},{1,5},{2,6},{3,7},{4,0},{5,1},{6,2},{7,3},{8,12},{9,13},{10,... | collective-permute-start | bytes 393224 | tf_op jit(solution)/shard_map/ppermute | solution.py:32
  102.9 9.0 %collective-permute-start.2 = (f32[1,2,16384]{2,1,0:T(2,128)S(1)}, f32[1,2,16384]{2,1,0:T(2,128)S(1)}, u32[]{:S(2)}, u32[]{:S(2)}) collective-permute-start(f32[1,2,16384]{2,1,0:T(2,128)S(1)} %broadcast_select_fusion.8), channel_id=1, source_target_pairs={{0,4},{1,5},{2,6},{3,7},{4,0},{5,1},{6,2},{7,3},{8,12},{9,13},{10,... | collective-permute-start | bytes 393224 | tf_op jit(solution)/shard_map/ppermute | solution.py:32
  105.8 6.3 %collective-permute-start.11 = (f32[1,1,16384]{2,1,0:T(1,128)S(1)}, f32[1,1,16384]{2,1,0:T(1,128)S(1)}, u32[]{:S(2)}, u32[]{:S(2)}) collective-permute-start(f32[1,1,16384]{2,1,0:T(1,128)S(1)} %get-tuple-element.13), channel_id=1, source_target_pairs={{0,1},{1,2},{2,3},{3,4},{4,5},{5,6},{6,7},{7,0},{8,9},{9,10},{10,1... | collective-permute-start | bytes 196616 | tf_op jit(solution)/shard_map/ppermute | solution.py:32
  108.6 5.2 %collective-permute-start.7 = (f32[1,1,16384]{2,1,0:T(1,128)S(1)}, f32[1,1,16384]{2,1,0:T(1,128)S(1)}, u32[]{:S(2)}, u32[]{:S(2)}) collective-permute-start(f32[1,1,16384]{2,1,0:T(1,128)S(1)} %get-tuple-element.15), channel_id=1, source_target_pairs={{0,1},{1,2},{2,3},{3,4},{4,5},{5,6},{6,7},{7,0},{8,9},{9,10},{10,1... | collective-permute-start | bytes 196616 | tf_op jit(solution)/shard_map/ppermute | solution.py:32
  112.0 17.1 %collective-permute-start.3 = (f32[1,1,16384]{2,1,0:T(1,128)S(1)}, f32[1,1,16384]{2,1,0:T(1,128)S(1)}, u32[]{:S(2)}, u32[]{:S(2)}) collective-permute-start(f32[1,1,16384]{2,1,0:T(1,128)S(1)} %get-tuple-element.17), channel_id=1, source_target_pairs={{0,1},{1,2},{2,3},{3,4},{4,5},{5,6},{6,7},{7,0},{8,9},{9,10},{10,1... | collective-permute-start | bytes 196616 | tf_op jit(solution)/shard_map/ppermute | solution.py:32
  112.3 32.9 %collective-permute-start.12 = (f32[1,2,16384]{2,1,0:T(2,128)S(1)}, f32[1,2,16384]{2,1,0:T(2,128)S(1)}, u32[]{:S(2)}, u32[]{:S(2)}) collective-permute-start(f32[1,2,16384]{2,1,0:T(2,128)S(1)} %get-tuple-element.11), channel_id=1, source_target_pairs={{0,24},{8,0},{16,8},{24,16},{1,25},{9,1},{17,9},{25,17},{2,26},{10... | collective-permute-start | bytes 393224 | tf_op jit(solution)/shard_map/ppermute | solution.py:15
  145.3 10.1 %collective-permute-start.13 = (f32[1,2,32768]{2,1,0:T(2,128)S(1)}, f32[1,2,32768]{2,1,0:T(2,128)S(1)}, u32[]{:S(2)}, u32[]{:S(2)}) collective-permute-start(f32[1,2,32768]{2,1,0:T(2,128)S(1)} %pad_maximum_fusion), channel_id=1, source_target_pairs={{0,16},{8,24},{16,0},{24,8},{1,17},{9,25},{17,1},{25,9},{2,18},{10... | collective-permute-start | bytes 786440 | tf_op jit(solution)/shard_map/ppermute | solution.py:15
Sparse Core Ops, SparseCore 0:
  12.9 70.8 all-reduce.2
